TPU v7x, 32 devices: a whole 2x2x4 slice. The times are simulated.
32 devices in a mesh: grp: 2 (over y), bus: 4 (over z), line: 2 (over x), scen: 2 (over core).
Axes of the slice: x: 2, y: 2, z: 4, core: 2. Of those that a mesh axis runs over, the one named last changes fastest.
Arguments:
- injections: float32 [128, 4, 4096], P(('grp', 'bus', 'scen'), None, 'line'), parts along dimension 0, may hold values from -6 to 6
- shift_factors: float32 [8192, 16384], P('line', 'bus'), may hold values from -0.046875 to 0.046875
- line_limits: int32 [8192], P('line'), may hold values from 20 to 149
- overload_cost: float32 [8192], P('line'), may hold values from 0.5 to 5
Outputs:
- line_flows: float32 [128, 8192], P(('grp', 'bus', 'scen'), 'line'), parts along dimension 0
- penalty_gradient: float32 [128, 4, 4096], P(('grp', 'bus', 'scen'), None, 'line'), parts along dimension 0
There are 2 independent parts, one for each index of `grp`. A program takes and returns all parts, laid end to end along the dimension named above; an argument that names none is the same for every part. Nothing has to cross between parts.
Inputs may be any that keep to these rules, and one draw needn't show every extreme that they name: `line_limits`: thermal limits in MW on a 100 MW base.
All inputs are finite; a program needn't handle non-finite values.
Results may differ from a plain program's by a relative error of at most 0.00011.
Values sent between devices are 32-bit elements; how exact they have to be, the bound alone decides.
No kernel may reach another device: no remote copies, remote signals or barrier semaphores. Data moves between devices by JAX's collectives and lax.ppermute only.
A program may use at most 128 MiB of HBM per device.

v0:
```python
import jax
import jax.numpy as jnp
from jax import lax
from jax.sharding import PartitionSpec as P


def contract_buses(values, factors):
    return lax.dot_general(
        values,
        factors,
        (((1,), (1,)), ((), ())),
        precision=lax.Precision.HIGHEST,
        preferred_element_type=jnp.float32,
    )


def penalty_slopes(flows_part, line_limits, overload_cost):
    limits = line_limits.astype(jnp.float32) / 100.0
    excess = jax.nn.relu(flows_part - limits) - jax.nn.relu(-flows_part - limits)
    return 2.0 * overload_cost * excess


def on_device(injections, shift_factors, line_limits, overload_cost):
    widened = lax.all_gather(injections, "line", axis=2, tiled=True)
    relayed = lax.all_to_all(widened, "bus", split_axis=1, concat_axis=0, tiled=True)
    partial_flows = contract_buses(relayed[:, 0, :], shift_factors)
    group_rows = partial_flows.shape[0]
    own_count = group_rows // lax.axis_size("bus")
    summed = lax.psum(partial_flows, "bus")
    group_slopes = penalty_slopes(summed, line_limits, overload_cost)
    line_flows = lax.dynamic_slice_in_dim(summed, lax.axis_index("bus") * own_count, own_count, 0)
    partial_grad = jnp.dot(
        group_slopes,
        shift_factors,
        precision=lax.Precision.HIGHEST,
        preferred_element_type=jnp.float32,
    )
    reduced = lax.psum_scatter(partial_grad, "line", scatter_dimension=1, tiled=True)
    penalty_gradient = lax.all_to_all(
        reduced[:, None, :], "bus", split_axis=0, concat_axis=1, tiled=True
    )
    return (line_flows, penalty_gradient)


def solution(mesh):
    in_specs = (P(("grp", "bus", "scen"), None, "line"), P("line", "bus"), P("line"), P("line"))
    out_specs = (P(("grp", "bus", "scen"), "line"), P(("grp", "bus", "scen"), None, "line"))
    return jax.shard_map(
        on_device, mesh=mesh, in_specs=in_specs, out_specs=out_specs, check_vma=False
    )
```

profile of v0, /device:TPU:0, one launch (start us, length us, event | category | flops | bytes accessed | tf_op | source)
XLA Modules:
  0.0 223.7 jit_solution(5629796355818969370)
XLA Ops:
  7.2 0.0 copy-start.1
  7.2 0.0 copy-start
  7.2 0.0 all-reduce.2.cloned.1.call-start
  7.2 1.1 copy.9
  8.3 9.9 %all_gather.3 = f32[8,4,4096]{2,0,1:T(8,128)S(1)} all-gather(f32[8,4,2048]{2,0,1:T(8,128)S(1)} %copy.9), channel_id=1, replica_groups=mesh['grp'=2,'bus'=4,'line'=2,'scen'=2] {'line'}, dimensions={2}, use_global_device_ids=true | all-gather | bytes 786432 | tf_op jit(solution)/shard_map/all_gather | solution.py:24
  18.3 18.5 %all_to_all.33 = f32[8,4,4096]{2,0,1:T(8,128)S(1)} all-to-all(f32[8,4,4096]{2,0,1:T(8,128)S(1)} %all_gather.3), channel_id=1, replica_groups=mesh['grp'=2,'bus'=4,'line'=2,'scen'=2] {'bus'}, dimensions={1} | all-to-all | bytes 1048576 | tf_op jit(solution)/shard_map/all_to_all | solution.py:25
  36.8 66.5 %fusion = f32[32,4096]{1,0:T(8,128)} fusion(f32[4096,4096]{1,0:T(8,128)} %param.5, f32[8,4,4096]{2,0,1:T(8,128)S(1)} %all_to_all.33), kind=kOutput, calls=%fused_computation | convolution fusion | flops 6442450944 | bytes 68157440 | tf_op jit(solution)/shard_map/dot_general | solution.py:8
  103.3 0.0 all-reduce.2.cloned.1.call-update
  103.4 0.2 reduce-scatter.2.cloned.1.call-start
  103.6 0.0 copy-done.1
  103.6 0.0 copy-done
  103.6 37.6 %all-reduce.2.cloned.1.call-done = f32[32,4096]{1,0:T(8,128)} async-done(((f32[32,4096]{1,0:T(8,128)}), f32[32,4096]{1,0:T(8,128)}) %all-reduce.2.cloned.1.call-update) | async-done | bytes 524304 | tf_op jit(solution)/shard_map/psum | solution.py:29
  141.2 44.9 %fusion.2 = f32[32,4096]{1,0:T(8,128)} fusion(f32[4096,4096]{1,0:T(8,128)} %param.5, f32[32,4096]{1,0:T(8,128)} %all-reduce.2.cloned.1.call-done, f32[4096]{0:T(1024)S(1)} %get-tuple-element.2, f32[4096]{0:T(1024)S(1)} %get-tuple-element.3), kind=kOutput, calls=%fused_computation.2 | convolution fusion | flops 6443368448 | bytes 68190208 | tf_op jit(solution)/shard_map/dot_general | solution.py:32
  186.1 0.0 reduce-scatter.2.cloned.1.call-update
  186.2 14.6 %reduce-scatter.2.cloned.1.call-done = f32[32,2048]{1,0:T(8,128)} async-done(((f32[32,4096]{1,0:T(8,128)}), f32[32,2048]{1,0:T(8,128)}) %reduce-scatter.2.cloned.1.call-update) | async-done | bytes 262160 | tf_op jit(solution)/shard_map/reduce_scatter | solution.py:38
  200.8 1.9 copy.10
  202.7 4.6 %all-to-all-start.1 = ((f32[32,1,2048]{2,1,0:T(1,128)}), f32[32,1,2048]{2,1,0:T(1,128)S(1)}, u32[]{:S(2)}, u32[]{:S(2)}) async-start(f32[32,1,2048]{2,1,0:T(1,128)} %copy.10), calls=%async_computation.2 | async-start | bytes 524288 | tf_op jit(solution)/shard_map/all_to_all | solution.py:39
  207.3 1.6 constant_dynamic-slice_fusion
  208.9 7.2 %all-to-all-done.1 = f32[32,1,2048]{2,1,0:T(1,128)S(1)} async-done(((f32[32,1,2048]{2,1,0:T(1,128)}), f32[32,1,2048]{2,1,0:T(1,128)S(1)}, u32[]{:S(2)}, u32[]{:S(2)}) %all-to-all-start.1) | async-done | bytes 262176 | tf_op jit(solution)/shard_map/all_to_all | solution.py:39
  216.0 0.9 copy.13
  (1 shorter events, 0.0 us)
Async XLA Ops:
  7.2 96.4 %copy-start.1 = (f32[4096]{0:T(1024)S(1)}, f32[4096]{0:T(1024)}, u32[]{:S(2)}) copy-start(f32[4096]{0:T(1024)} %param.7) | copy-start | bytes 49156
  7.2 96.4 %copy-start = (s32[4096]{0:T(1024)S(1)}, s32[4096]{0:T(1024)}, u32[]{:S(2)}) copy-start(s32[4096]{0:T(1024)} %param.6) | copy-start | bytes 49156
  7.2 134.0 %all-reduce.2.cloned.1.call-start = ((), (), s32[]{:S(2)}) async-start(), calls=%async_computation.3 | async-start | bytes 1048576 | tf_op jit(solution)/shard_map/psum | solution.py:29
  103.4 97.4 %reduce-scatter.2.cloned.1.call-start = ((), (), s32[]{:S(2)}) async-start(), calls=%async_computation.4 | async-start | bytes 786432 | tf_op jit(solution)/shard_map/reduce_scatter | solution.py:38
  202.7 13.3 %all-to-all-start.1 = ((f32[32,1,2048]{2,1,0:T(1,128)}), f32[32,1,2048]{2,1,0:T(1,128)S(1)}, u32[]{:S(2)}, u32[]{:S(2)}) async-start(f32[32,1,2048]{2,1,0:T(1,128)} %copy.10), calls=%async_computation.2 | async-start | bytes 524288 | tf_op jit(solution)/shard_map/all_to_all | solution.py:39
Sparse Core Ops, SparseCore 0:
  103.5 37.6 all-reduce.1
  186.3 14.4 reduce-scatter.1
where the time goes:
time: 224 us
  matrix products  111 us (50%)
  waiting for transfers between devices  59.4 us (27%)
  blocking collectives  28.5 us (13%)
  between operations  14.1 us (6%)
  local copies, waits for them, and re-layouts  5.48 us (2%)
  starting transfers between devices  4.85 us (2%)
    dot_general x1, matrix products, contract_buses(): lax.dot_general(values, factors, (((1,), (1,)), ((), ())), precision=lax....  66.5 us
    dot_general x1, matrix products, on_device(): jnp.dot(group_slopes, shift_factors, precision=lax.Precision.HIGHEST, pre...  44.9 us
    psum x1, waiting for transfers between devices, on_device(): summed = lax.psum(partial_flows, 'bus')  37.6 us
    all_to_all x1, blocking collectives, on_device(): lax.all_to_all(widened, 'bus', split_axis=1, concat_axis=0, tiled=True)  18.5 us
    reduce_scatter x1, waiting for transfers between devices, on_device(): lax.psum_scatter(partial_grad, 'line', scatter_dimension=1, tiled=True)  14.6 us
    all_gather x1, blocking collectives, on_device(): widened = lax.all_gather(injections, 'line', axis=2, tiled=True)  9.94 us
    all_to_all x1, waiting for transfers between devices, on_device(): lax.all_to_all(reduced[:, None, :], 'bus', split_axis=0, concat_axis=1, t...  7.16 us
    all_to_all x1, starting transfers between devices, on_device(): lax.all_to_all(reduced[:, None, :], 'bus', split_axis=0, concat_axis=1, t...  4.59 us
  transfers between devices with their start and end apart: 3, of which 3 were waited for; matrix products, arithmetic and copies ran while one was open for 1% of the time, Pallas kernels for 0%

commit v1 on v0

--- a/solution.py
+++ b/solution.py
@@ -26,7 +26,7 @@
     partial_flows = contract_buses(relayed[:, 0, :], shift_factors)
     group_rows = partial_flows.shape[0]
     own_count = group_rows // lax.axis_size("bus")
-    summed = lax.psum(partial_flows, "bus")
+    summed = jnp.sum(lax.all_gather(partial_flows, "bus"), axis=0)
     group_slopes = penalty_slopes(summed, line_limits, overload_cost)
     line_flows = lax.dynamic_slice_in_dim(summed, lax.axis_index("bus") * own_count, own_count, 0)
     partial_grad = jnp.dot(

time: 224 us -> 232 us (1.036)
  waiting for transfers between devices: 59.4 us -> 66.4 us
    all_gather x0 -> x1, waiting for transfers between devices: none -> 44.7 us  [on_device(): summed = jnp.sum(lax.all_gather(partial_flows, 'bus'), axis=0)]
    psum x1 -> x0, waiting for transfers between devices: 37.6 us -> none  [on_device(): summed = lax.psum(partial_flows, 'bus')]
  transfers between devices with their start and end apart: 3 -> 3, of which waited for: 3 -> 3; matrix products, arithmetic and copies ran while one was open for 1% -> 0% of each run, Pallas kernels for 0% -> 0%
where the time goes in v1:
time: 232 us
  matrix products  111 us (48%)
  waiting for transfers between devices  66.4 us (29%)
  blocking collectives  28.5 us (12%)
  between operations  14.1 us (6%)
  starting transfers between devices  4.85 us (2%)
  local copies, waits for them, and re-layouts  4.57 us (2%)
    dot_general x1, matrix products, contract_buses(): lax.dot_general(values, factors, (((1,), (1,)), ((), ())), precision=lax....  66.5 us
    dot_general x1, matrix products, on_device(): jnp.dot(group_slopes, shift_factors, precision=lax.Precision.HIGHEST, pre...  44.9 us
    all_gather x1, waiting for transfers between devices, on_device(): summed = jnp.sum(lax.all_gather(partial_flows, 'bus'), axis=0)  44.7 us
    all_to_all x1, blocking collectives, on_device(): lax.all_to_all(widened, 'bus', split_axis=1, concat_axis=0, tiled=True)  18.5 us
    reduce_scatter x1, waiting for transfers between devices, on_device(): lax.psum_scatter(partial_grad, 'line', scatter_dimension=1, tiled=True)  13.6 us
    all_gather x1, blocking collectives, on_device(): widened = lax.all_gather(injections, 'line', axis=2, tiled=True)  9.94 us
    all_to_all x1, waiting for transfers between devices, on_device(): lax.all_to_all(reduced[:, None, :], 'bus', split_axis=0, concat_axis=1, t...  8.08 us
  transfers between devices with their start and end apart: 3, of which 3 were waited for; matrix products, arithmetic and copies ran while one was open for 0% of the time, Pallas kernels for 0%

profile of v1, /device:TPU:0, one launch (start us, length us, event | category | flops | bytes accessed | tf_op | source)
XLA Modules:
  0.0 231.6 jit_solution(8070750827019095575)
XLA Ops:
  7.2 0.0 copy-start
  7.2 0.0 copy-start.1
  7.2 0.0 all-gather.3.cloned.1.call-start
  7.2 1.1 copy.9
  8.3 9.9 %all_gather.9 = f32[8,4,4096]{2,0,1:T(8,128)S(1)} all-gather(f32[8,4,2048]{2,0,1:T(8,128)S(1)} %copy.9), channel_id=1, replica_groups=mesh['grp'=2,'bus'=4,'line'=2,'scen'=2] {'line'}, dimensions={2}, use_global_device_ids=true | all-gather | bytes 786432 | tf_op jit(solution)/shard_map/all_gather | solution.py:24
  18.3 18.5 %all_to_all.33 = f32[8,4,4096]{2,0,1:T(8,128)S(1)} all-to-all(f32[8,4,4096]{2,0,1:T(8,128)S(1)} %all_gather.9), channel_id=1, replica_groups=mesh['grp'=2,'bus'=4,'line'=2,'scen'=2] {'bus'}, dimensions={1} | all-to-all | bytes 1048576 | tf_op jit(solution)/shard_map/all_to_all | solution.py:25
  36.8 66.5 %fusion = f32[32,4096]{1,0:T(8,128)} fusion(f32[4096,4096]{1,0:T(8,128)} %param.5, f32[8,4,4096]{2,0,1:T(8,128)S(1)} %all_to_all.33), kind=kOutput, calls=%fused_computation | convolution fusion | flops 6442450944 | bytes 68157440 | tf_op jit(solution)/shard_map/dot_general | solution.py:8
  103.3 0.0 all-gather.3.cloned.1.call-update
  103.4 0.2 reduce-scatter.2.cloned.1.call-start
  103.6 0.0 copy-done
  103.6 0.0 copy-done.1
  103.6 44.7 %all-gather.3.cloned.1.call-done = f32[128,4096]{1,0:T(8,128)} async-done(((f32[32,4096]{1,0:T(8,128)}), f32[128,4096]{1,0:T(8,128)}) %all-gather.3.cloned.1.call-update) | async-done | bytes 2097168 | tf_op jit(solution)/shard_map/all_gather | solution.py:29
  148.3 1.8 reduce_sum.9
  150.1 44.9 %fusion.2 = f32[32,4096]{1,0:T(8,128)} fusion(f32[4096,4096]{1,0:T(8,128)} %param.5, f32[32,4096]{1,0:T(8,128)S(1)} %reduce_sum.9, f32[4096]{0:T(1024)S(1)} %get-tuple-element.2, f32[4096]{0:T(1024)S(1)} %get-tuple-element.3), kind=kOutput, calls=%fused_computation.2 | convolution fusion | flops 6443368448 | bytes 68190208 | tf_op jit(solution)/shard_map/dot_general | solution.py:32
  195.0 0.0 reduce-scatter.2.cloned.1.call-update
  195.0 13.6 %reduce-scatter.2.cloned.1.call-done = f32[32,2048]{1,0:T(8,128)} async-done(((f32[32,4096]{1,0:T(8,128)}), f32[32,2048]{1,0:T(8,128)}) %reduce-scatter.2.cloned.1.call-update) | async-done | bytes 262160 | tf_op jit(solution)/shard_map/reduce_scatter | solution.py:38
  208.6 1.9 copy.10
  210.5 4.6 %all-to-all-start.1 = ((f32[32,1,2048]{2,1,0:T(1,128)}), f32[32,1,2048]{2,1,0:T(1,128)S(1)}, u32[]{:S(2)}, u32[]{:S(2)}) async-start(f32[32,1,2048]{2,1,0:T(1,128)} %copy.10), calls=%async_computation.2 | async-start | bytes 524288 | tf_op jit(solution)/shard_map/all_to_all | solution.py:39
  215.1 0.7 constant_dynamic-slice_fusion
  215.8 8.1 %all-to-all-done.1 = f32[32,1,2048]{2,1,0:T(1,128)S(1)} async-done(((f32[32,1,2048]{2,1,0:T(1,128)}), f32[32,1,2048]{2,1,0:T(1,128)S(1)}, u32[]{:S(2)}, u32[]{:S(2)}) %all-to-all-start.1) | async-done | bytes 262176 | tf_op jit(solution)/shard_map/all_to_all | solution.py:39
  223.9 0.9 copy.13
  (1 shorter events, 0.0 us)
Async XLA Ops:
  7.2 96.4 %copy-start = (s32[4096]{0:T(1024)S(1)}, s32[4096]{0:T(1024)}, u32[]{:S(2)}) copy-start(s32[4096]{0:T(1024)} %param.6) | copy-start | bytes 49156
  7.2 96.4 %copy-start.1 = (f32[4096]{0:T(1024)S(1)}, f32[4096]{0:T(1024)}, u32[]{:S(2)}) copy-start(f32[4096]{0:T(1024)} %param.7) | copy-start | bytes 49156
  7.2 141.1 %all-gather.3.cloned.1.call-start = ((), (), s32[]{:S(2)}) async-start(), calls=%async_computation.4 | async-start | bytes 2621440 | tf_op jit(solution)/shard_map/all_gather | solution.py:29
  103.4 105.3 %reduce-scatter.2.cloned.1.call-start = ((), (), s32[]{:S(2)}) async-start(), calls=%async_computation.3 | async-start | bytes 786432 | tf_op jit(solution)/shard_map/reduce_scatter | solution.py:38
  210.5 13.3 %all-to-all-start.1 = ((f32[32,1,2048]{2,1,0:T(1,128)}), f32[32,1,2048]{2,1,0:T(1,128)S(1)}, u32[]{:S(2)}, u32[]{:S(2)}) async-start(f32[32,1,2048]{2,1,0:T(1,128)} %copy.10), calls=%async_computation.2 | async-start | bytes 524288 | tf_op jit(solution)/shard_map/all_to_all | solution.py:39
Sparse Core Ops, SparseCore 0:
  103.5 44.7 all-gather.2
  195.2 13.4 reduce-scatter.1

commit v2 on v0

--- a/solution.py
+++ b/solution.py
@@ -22,7 +22,10 @@
 
 def on_device(injections, shift_factors, line_limits, overload_cost):
     widened = lax.all_gather(injections, "line", axis=2, tiled=True)
-    relayed = lax.all_to_all(widened, "bus", split_axis=1, concat_axis=0, tiled=True)
+    relayed = jnp.concatenate(
+        lax.all_to_all(jnp.stack(jnp.split(widened, lax.axis_size("bus"), axis=1)), "bus", 0, 0),
+        axis=0,
+    )
     partial_flows = contract_buses(relayed[:, 0, :], shift_factors)
     group_rows = partial_flows.shape[0]
     own_count = group_rows // lax.axis_size("bus")

time: 224 us -> 225 us (level)
  no operation moved by 1% of the time
where the time goes in v2:
time: 225 us
  matrix products  112 us (50%)
  waiting for transfers between devices  59.3 us (26%)
  blocking collectives  28.7 us (13%)
  between operations  14.1 us (6%)
  starting transfers between devices  4.85 us (2%)
  local copies, waits for them, and re-layouts  4.81 us (2%)
    dot_general x1, matrix products, contract_buses(): lax.dot_general(values, factors, (((1,), (1,)), ((), ())), precision=lax....  67.3 us
    dot_general x1, matrix products, on_device(): jnp.dot(group_slopes, shift_factors, precision=lax.Precision.HIGHEST, pre...  44.9 us
    psum x1, waiting for transfers between devices, on_device(): summed = lax.psum(partial_flows, 'bus')  37.5 us
    all_to_all x1, blocking collectives, on_device(): lax.all_to_all(jnp.stack(jnp.split(widened, lax.axis_size('bus'), axis=1)...  18.5 us
    reduce_scatter x1, waiting for transfers between devices, on_device(): lax.psum_scatter(partial_grad, 'line', scatter_dimension=1, tiled=True)  14.6 us
    all_gather x1, blocking collectives, on_device(): widened = lax.all_gather(injections, 'line', axis=2, tiled=True)  10.2 us
    all_to_all x1, waiting for transfers between devices, on_device(): lax.all_to_all(reduced[:, None, :], 'bus', split_axis=0, concat_axis=1, t...  7.16 us
    all_to_all x1, starting transfers between devices, on_device(): lax.all_to_all(reduced[:, None, :], 'bus', split_axis=0, concat_axis=1, t...  4.59 us
  transfers between devices with their start and end apart: 3, of which 3 were waited for; matrix products, arithmetic and copies ran while one was open for 1% of the time, Pallas kernels for 0%

profile of v2, /device:TPU:0, one launch (start us, length us, event | category | flops | bytes accessed | tf_op | source)
XLA Modules:
  0.0 224.6 jit_solution(3707033856214736309)
XLA Ops:
  7.2 0.0 copy-start.1
  7.2 0.0 copy-start
  7.2 0.0 all-reduce.2.cloned.1.call-start
  7.2 10.2 %all_gather.3 = f32[8,4,4096]{2,1,0:T(4,128)S(1)} all-gather(f32[8,4,2048]{2,1,0:T(4,128)} %param.4), channel_id=1, replica_groups=mesh['grp'=2,'bus'=4,'line'=2,'scen'=2] {'line'}, dimensions={2}, use_global_device_ids=true | all-gather | bytes 786432 | tf_op jit(solution)/shard_map/all_gather | solution.py:24
  17.4 0.4 slice_bitcast_fusion.3
  17.9 0.5 pad_maximum_fusion
  18.4 18.5 %all_to_all.23 = f32[4,8,1,4096]{3,2,1,0:T(1,128)S(1)} all-to-all(f32[4,8,1,4096]{3,2,1,0:T(1,128)S(1)} %pad_maximum_fusion), channel_id=1, replica_groups=mesh['grp'=2,'bus'=4,'line'=2,'scen'=2] {'bus'}, dimensions={0} | all-to-all | bytes 1048576 | tf_op jit(solution)/shard_map/all_to_all | solution.py:26
  36.9 67.3 %fusion = f32[32,4096]{1,0:T(8,128)} fusion(f32[4096,4096]{1,0:T(8,128)} %param.5, f32[4,8,1,4096]{3,2,1,0:T(1,128)S(1)} %all_to_all.23), kind=kOutput, calls=%fused_computation.1 | convolution fusion | flops 6442450944 | bytes 68157440 | tf_op jit(solution)/shard_map/dot_general | solution.py:8
  104.2 0.0 all-reduce.2.cloned.1.call-update
  104.3 0.2 reduce-scatter.2.cloned.1.call-start
  104.5 0.0 copy-done.1
  104.5 0.0 copy-done
  104.5 37.5 %all-reduce.2.cloned.1.call-done = f32[32,4096]{1,0:T(8,128)} async-done(((f32[32,4096]{1,0:T(8,128)}), f32[32,4096]{1,0:T(8,128)}) %all-reduce.2.cloned.1.call-update) | async-done | bytes 524304 | tf_op jit(solution)/shard_map/psum | solution.py:32
  142.1 44.9 %fusion.3 = f32[32,4096]{1,0:T(8,128)} fusion(f32[4096,4096]{1,0:T(8,128)} %param.5, f32[32,4096]{1,0:T(8,128)} %all-reduce.2.cloned.1.call-done, f32[4096]{0:T(1024)S(1)} %get-tuple-element.6, f32[4096]{0:T(1024)S(1)} %get-tuple-element.7), kind=kOutput, calls=%fused_computation.4 | convolution fusion | flops 6443368448 | bytes 68190208 | tf_op jit(solution)/shard_map/dot_general | solution.py:35
  187.0 0.0 reduce-scatter.2.cloned.1.call-update
  187.0 14.6 %reduce-scatter.2.cloned.1.call-done = f32[32,2048]{1,0:T(8,128)} async-done(((f32[32,4096]{1,0:T(8,128)}), f32[32,2048]{1,0:T(8,128)}) %reduce-scatter.2.cloned.1.call-update) | async-done | bytes 262160 | tf_op jit(solution)/shard_map/reduce_scatter | solution.py:41
  201.6 1.9 copy.7
  203.6 4.6 %all-to-all-start.1 = ((f32[32,1,2048]{2,1,0:T(1,128)}), f32[32,1,2048]{2,1,0:T(1,128)S(1)}, u32[]{:S(2)}, u32[]{:S(2)}) async-start(f32[32,1,2048]{2,1,0:T(1,128)} %copy.7), calls=%async_computation.2 | async-start | bytes 524288 | tf_op jit(solution)/shard_map/all_to_all | solution.py:42
  208.2 1.6 constant_dynamic-slice_fusion
  209.7 7.2 %all-to-all-done.1 = f32[32,1,2048]{2,1,0:T(1,128)S(1)} async-done(((f32[32,1,2048]{2,1,0:T(1,128)}), f32[32,1,2048]{2,1,0:T(1,128)S(1)}, u32[]{:S(2)}, u32[]{:S(2)}) %all-to-all-start.1) | async-done | bytes 262176 | tf_op jit(solution)/shard_map/all_to_all | solution.py:42
  216.9 0.9 copy.15
  (1 shorter events, 0.0 us)
Async XLA Ops:
  7.2 97.3 %copy-start.1 = (f32[4096]{0:T(1024)S(1)}, f32[4096]{0:T(1024)}, u32[]{:S(2)}) copy-start(f32[4096]{0:T(1024)} %param.7) | copy-start | bytes 49156
  7.2 97.3 %copy-start = (s32[4096]{0:T(1024)S(1)}, s32[4096]{0:T(1024)}, u32[]{:S(2)}) copy-start(s32[4096]{0:T(1024)} %param.6) | copy-start | bytes 49156
  7.2 134.9 %all-reduce.2.cloned.1.call-start = ((), (), s32[]{:S(2)}) async-start(), calls=%async_computation.3 | async-start | bytes 1048576 | tf_op jit(solution)/shard_map/psum | solution.py:32
  104.3 97.4 %reduce-scatter.2.cloned.1.call-start = ((), (), s32[]{:S(2)}) async-start(), calls=%async_computation.4 | async-start | bytes 786432 | tf_op jit(solution)/shard_map/reduce_scatter | solution.py:41
  203.6 13.3 %all-to-all-start.1 = ((f32[32,1,2048]{2,1,0:T(1,128)}), f32[32,1,2048]{2,1,0:T(1,128)S(1)}, u32[]{:S(2)}, u32[]{:S(2)}) async-start(f32[32,1,2048]{2,1,0:T(1,128)} %copy.7), calls=%async_computation.2 | async-start | bytes 524288 | tf_op jit(solution)/shard_map/all_to_all | solution.py:42
Sparse Core Ops, SparseCore 0:
  104.4 37.6 all-reduce.1
  187.2 14.4 reduce-scatter.1
